TPU v7x, 128 devices: a whole 4x4x4 slice. The times are simulated.
128 devices in a mesh: rep: 8 (over z_lo, x), tp: 16 (over y, z_hi, core).
Axes of the slice: x: 4, y: 4, z: 4 (z_hi: 2, z_lo: 2; z = z_hi * 2 + z_lo), core: 2. Of those that a mesh axis runs over, the one named last changes fastest.
Arguments:
- batch_rows: bfloat16 [12288, 4096], P(('rep', 'tp')), may hold values from -6 to 6
- token_slots: int32 [8, 384], P('rep'), may hold values from 0 to 1535, as said below
- holder_map: int32 [8, 16], P('rep'), may hold values from -2 to 111, as said below
- copies: bfloat16 [32768, 16384], P('rep', 'tp'), may hold values from -6 to 6
- upstream: bfloat16 [3072, 16384], P('rep', 'tp'), may hold values from -18 to 18
- up_act: bfloat16 [3072, 16384], P('rep', 'tp'), may hold values from -6 to 6
- master: float32 [4096, 14336], P('rep', 'tp'), may hold values from -0.078125 to 0.078125
- moment1: bfloat16 [4096, 14336], P('rep', 'tp'), may hold values from -0.75 to 0.75
- moment2: bfloat16 [4096, 14336], P('rep', 'tp'), may hold values from 0.049804688 to 2
Outputs:
- master_next: float32 [4096, 14336], P('rep', 'tp')
- moment1_next: bfloat16 [4096, 14336], P('rep', 'tp')
- moment2_next: bfloat16 [4096, 14336], P('rep', 'tp')
- copy_next: bfloat16 [32768, 16384], P('rep', 'tp')
Inputs may be any that keep to these rules, and one draw needn't show every extreme that they name: `token_slots`: row r lists 384 distinct rows of replica r's batch. `holder_map`: each row is one replica. A row is either -1 everywhere, or holds -2 at exactly 2 devices and at every other device a distinct piece 7 * j + s (0 <= s < 7) with j one of that row's -2 devices, each such piece exactly once. 4 rows are of the second kind. Columns of copies, upstream and up_act that the steps do not name are not read.
All inputs are finite; a program needn't handle non-finite values.
Results may differ from a plain program's by a relative error of at most 0.02.
Values may be sent and summed in bfloat16 or wider, within the bound.
A program may use at most 128 MiB of HBM per device.

v0:
```python
import math
import jax
import jax.numpy as jnp
from jax import lax
from jax.sharding import PartitionSpec as P

beta_one = 0.9
beta_two = 0.95
bias_one = 1.0 - 0.9**10
bias_two = 1.0 - 0.95**10
learn_rate = 0.05
weight_decay = 0.1
epsilon = 1e-08


def picked(indices, table):
    one_hot = (indices[:, None] == jnp.arange(table.shape[0], dtype=jnp.int32)[None, :]).astype(
        jnp.bfloat16
    )
    return jnp.dot(one_hot, table, preferred_element_type=jnp.float32).astype(jnp.bfloat16)


def on_device(
    batch_rows, token_slots, holder_map, copies, upstream, up_act, master, moment1, moment2
):
    tp_count = lax.axis_size("tp")
    rep_count = lax.axis_size("rep")
    position = lax.axis_index("tp")
    holders = holder_map[0]
    own_entry = jnp.sum(jnp.where(jnp.arange(tp_count) == position, holders, 0))
    all_holders = lax.all_gather(holders, "rep")
    unit_cols = copies.shape[1] // 8
    wide_cols = 7 * unit_cols
    scaling = 1.0 / math.sqrt(copies.shape[0])
    columns = lax.all_to_all(batch_rows, "tp", split_axis=1, concat_axis=0, tiled=True)
    chosen = picked(token_slots[0], columns)
    inputs = lax.all_gather(chosen, "tp", axis=1, tiled=True)
    gate_pre = jnp.dot(inputs, copies, preferred_element_type=jnp.float32) * scaling
    logistic = jax.nn.sigmoid(gate_pre)
    gate_grad = (
        upstream.astype(jnp.float32)
        * up_act.astype(jnp.float32)
        * logistic
        * (1.0 + gate_pre * (1.0 - logistic))
    ).astype(jnp.bfloat16)
    tokens = gate_grad.shape[0]
    pooled = lax.all_to_all(
        jnp.broadcast_to(gate_grad[:, wide_cols:], (tp_count, tokens, unit_cols)),
        "tp",
        split_axis=0,
        concat_axis=0,
        tiled=True,
    )
    wanted = position * 7 + jnp.arange(7, dtype=jnp.int32)
    choice = (holders[None, :] == wanted[:, None]).astype(jnp.bfloat16)
    rebuilt = jnp.concatenate(
        [
            jnp.sum(jnp.where(choice[s, :, None, None] > 0, pooled, jnp.zeros_like(pooled)), axis=0)
            for s in range(7)
        ],
        axis=1,
    )
    block_grad = jnp.where(own_entry == -2, rebuilt, gate_grad[:, :wide_cols])
    product = lax.dot_general(
        inputs, block_grad, (((0,), (0,)), ((), ())), preferred_element_type=jnp.float32
    )
    gradient = lax.psum_scatter(
        (product * scaling).astype(jnp.bfloat16), "rep", scatter_dimension=0, tiled=True
    ).astype(jnp.float32)
    first_new = beta_one * moment1.astype(jnp.float32) + (1.0 - beta_one) * gradient
    second_new = beta_two * moment2.astype(jnp.float32) + (1.0 - beta_two) * gradient * gradient
    step_size = first_new / bias_one / (jnp.sqrt(second_new / bias_two) + epsilon)
    master_next = master - learn_rate * (step_size + weight_decay * master)
    fresh = master_next.astype(jnp.bfloat16)
    full_block = lax.all_gather(fresh, "rep", axis=0, tiled=True)
    own_rows = fresh.shape[0]
    strip = own_rows // tp_count
    spread = lax.all_to_all(fresh, "tp", split_axis=0, concat_axis=0, tiled=True)
    table = spread.reshape(tp_count, strip, 7, unit_cols).transpose(0, 2, 1, 3)
    routed = picked(all_holders.reshape(-1), table.reshape(tp_count * 7, strip * unit_cols))
    routed = routed.reshape(rep_count, tp_count, strip, unit_cols)
    routed = lax.all_to_all(routed, "tp", split_axis=1, concat_axis=2, tiled=True)
    routed = routed.reshape(rep_count * own_rows, unit_cols)
    adopted = lax.all_to_all(routed, "rep", split_axis=0, concat_axis=0, tiled=True)
    copy_next = jnp.concatenate([full_block, adopted], axis=1)
    copy_next = jnp.where(own_entry == -2, jnp.zeros_like(copy_next), copy_next)
    return (master_next, first_new.astype(jnp.bfloat16), second_new.astype(jnp.bfloat16), copy_next)


def solution(mesh):
    placed = (
        P(("rep", "tp"), None),
        P("rep", None),
        P("rep", None),
        P("rep", "tp"),
        P("rep", "tp"),
        P("rep", "tp"),
        P("rep", "tp"),
        P("rep", "tp"),
        P("rep", "tp"),
    )
    return jax.shard_map(
        on_device,
        mesh=mesh,
        in_specs=placed,
        out_specs=(P("rep", "tp"), P("rep", "tp"), P("rep", "tp"), P("rep", "tp")),
        check_vma=False,
    )
```

profile of v0, /device:TPU:0, one launch (start us, length us, event | category | flops | bytes accessed | tf_op | source)
XLA Modules:
  0.0 366.0 jit_solution(13121369228132547831)
XLA Ops:
  7.2 0.0 copy-start.3
  7.2 2.1 copy.35
  9.3 0.0 copy-start.5
  9.3 0.0 copy-start.6
  9.3 8.1 %all-to-all-start = ((bf16[96,16,256]{2,0,1:T(8,128)(2,1)}), bf16[96,16,256]{2,0,1:T(8,128)(2,1)S(1)}, u32[]{:S(2)}, u32[]{:S(2)}) async-start(bf16[96,16,256]{2,0,1:T(8,128)(2,1)} %bitcast.40), calls=%async_computation | async-start | bytes 1572864 | tf_op jit(solution)/shard_map/all_to_all | solution.py:35
  17.4 0.0 all-gather.4.cloned.1.call-start
  17.4 0.0 copy-done.3
  17.5 15.1 %all-to-all-done = bf16[96,16,256]{2,0,1:T(8,128)(2,1)S(1)} async-done(((bf16[96,16,256]{2,0,1:T(8,128)(2,1)}), bf16[96,16,256]{2,0,1:T(8,128)(2,1)S(1)}, u32[]{:S(2)}, u32[]{:S(2)}) %all-to-all-start) | async-done | bytes 786464 | tf_op jit(solution)/shard_map/all_to_all | solution.py:35
  32.6 1.2 fusion.7
  33.8 0.0 all-gather.4.cloned.1.call-update
  33.8 51.7 %all-gather.4.cloned.1.call-done = bf16[384,4096]{1,0:T(8,128)(2,1)} async-done(((bf16[384,256]{1,0:T(8,128)(2,1)}), bf16[384,4096]{1,0:T(8,128)(2,1)}) %all-gather.4.cloned.1.call-update) | async-done | bytes 3145744 | tf_op jit(solution)/shard_map/all_gather | solution.py:37
  85.6 0.0 copy-done.5
  85.6 0.0 copy-done.6
  85.6 8.3 %multiply_convert_fusion.1 = bf16[384,1024]{1,0:T(8,128)(2,1)S(1)} fusion(bf16[384,1024]{1,0:T(8,128)(2,1)S(1)} %copy-done.5, bf16[384,1024]{1,0:T(8,128)(2,1)S(1)} %copy-done.6, bf16[384,4096]{1,0:T(8,128)(2,1)} %all-gather.4.cloned.1.call-done, bf16[4096,1024]{1,0:T(8,128)(2,1)} %param.12), kind=kOutput, calls=%fused_computation.17 | convolution fusion | flops 3226337280 | bytes 13893632 | tf_op jit(solution)/shard_map/dot_general | solution.py:38
  93.9 1.4 broadcast_in_dim.53
  95.3 0.0 copy-start.2
  95.3 3.9 %all-to-all-start.1 = ((bf16[16,384,128]{2,1,0:T(8,128)(2,1)}), bf16[16,384,128]{2,1,0:T(8,128)(2,1)S(1)}, u32[]{:S(2)}, u32[]{:S(2)}) async-start(bf16[16,384,128]{2,1,0:T(8,128)(2,1)} %broadcast_in_dim.53), calls=%async_computation.1 | async-start | bytes 3145728 | tf_op jit(solution)/shard_map/all_to_all | solution.py:47
  99.2 0.0 reduce-scatter.2.cloned.1.call-start
  99.3 0.0 copy-done.2
  99.3 0.6 fusion.12
  100.6 0.1 compare_convert_fusion
  100.6 22.1 %all-to-all-done.1 = bf16[16,384,128]{2,1,0:T(8,128)(2,1)S(1)} async-done(((bf16[16,384,128]{2,1,0:T(8,128)(2,1)}), bf16[16,384,128]{2,1,0:T(8,128)(2,1)S(1)}, u32[]{:S(2)}, u32[]{:S(2)}) %all-to-all-start.1) | async-done | bytes 1572896 | tf_op jit(solution)/shard_map/all_to_all | solution.py:47
  122.8 0.0 copy-start.4
  122.8 3.0 select_reduce_fusion
  126.0 0.0 copy-done.4
  126.0 6.4 %multiply_convert_fusion = bf16[4096,896]{1,0:T(8,128)(2,1)} fusion(bf16[384,4096]{1,0:T(8,128)(2,1)S(1)} %copy-done.4, bf16[384,896]{1,0:T(8,128)(2,1)S(1)} %constant_dynamic-update-slice_fusion, bf16[384,1024]{1,0:T(8,128)(2,1)S(1)} %multiply_convert_fusion.1, pred[]{:T(512)S(6)} %eq.59), kind=kOutput, calls=%fused_computation | convolution fusion | flops 2826256384 | bytes 11862017 | tf_op jit(solution)/shard_map/dot_general | solution.py:64
  132.4 0.0 copy-start
  132.4 0.0 copy-start.1
  132.4 0.0 reduce-scatter.2.cloned.1.call-update
  132.5 0.0 all-gather.6.cloned.1.call-start
  132.5 81.7 %reduce-scatter.2.cloned.1.call-done = bf16[512,896]{1,0:T(8,128)(2,1)} async-done(((bf16[4096,896]{1,0:T(8,128)(2,1)}), bf16[512,896]{1,0:T(8,128)(2,1)}) %reduce-scatter.2.cloned.1.call-update) | async-done | bytes 917520 | tf_op jit(solution)/shard_map/reduce_scatter | solution.py:67
  214.3 0.0 copy-done
  214.3 0.0 copy-done.1
  214.3 5.7 %fusion.13 = (bf16[512,896]{1,0:T(8,128)(2,1)}, f32[512,896]{1,0:T(8,128)}, bf16[512,896]{1,0:T(8,128)(2,1)}, bf16[512,896]{1,0:T(8,128)(2,1)}) fusion(f32[512,896]{1,0:T(8,128)S(1)} %copy-done, bf16[512,896]{1,0:T(8,128)(2,1)S(1)} %copy-done.1, bf16[512,896]{1,0:T(8,128)(2,1)} %reduce-scatter.2.cloned.1.call-done, bf16[512,896]{1,0:T(8,128)(2,1)} %param.16), kind=kLoop, calls=%fused_computation.48 | loop fusion | flops 9633792 | bytes 9175040 | tf_op jit(solution)/shard_map/convert_element_type | solution.py:74
  220.0 0.0 all-gather.6.cloned.1.call-update
  220.0 6.7 %all-to-all-start.2 = ((bf16[16,32,896]{2,1,0:T(8,128)(2,1)}), bf16[16,32,896]{2,1,0:T(8,128)(2,1)S(1)}, u32[]{:S(2)}, u32[]{:S(2)}) async-start(bf16[16,32,896]{2,1,0:T(8,128)(2,1)} %bitcast.41), calls=%async_computation.3 | async-start | bytes 1835008 | tf_op jit(solution)/shard_map/all_to_all | solution.py:78
  226.7 20.7 %all-gather = s32[8,1,16]{2,1,0:T(1,128)S(1)} all-gather(s32[1,1,16]{2,1,0:T(1,128)S(1)} %bitcast.50), channel_id=1, replica_groups=mesh['rep'=8,'tp'=16] {'rep'}, dimensions={0}, use_global_device_ids=true | all-gather | bytes 576 | tf_op jit(solution)/shard_map/all_gather | solution.py:31
  247.4 0.6 broadcast.92
  248.0 0.7 reduce.11
  248.7 0.1 eq.63
  248.8 60.8 %all-to-all-done.2 = bf16[16,32,896]{2,1,0:T(8,128)(2,1)S(1)} async-done(((bf16[16,32,896]{2,1,0:T(8,128)(2,1)}), bf16[16,32,896]{2,1,0:T(8,128)(2,1)S(1)}, u32[]{:S(2)}, u32[]{:S(2)}) %all-to-all-start.2) | async-done | bytes 917536 | tf_op jit(solution)/shard_map/all_to_all | solution.py:78
  309.6 1.0 reshape.100
  310.6 0.2 copy.24
  310.8 0.5 fusion.5
  311.3 0.2 copy.29
  311.5 0.1 copy.25
  311.7 22.6 %all_to_all.54 = bf16[8,16,32,128]{3,2,0,1:T(8,128)(2,1)S(1)} all-to-all(bf16[8,16,32,128]{3,2,0,1:T(8,128)(2,1)S(1)} %copy.25), channel_id=1, replica_groups=mesh['rep'=8,'tp'=16] {'tp'}, dimensions={1} | all-to-all | bytes 2097152 | tf_op jit(solution)/shard_map/all_to_all | solution.py:82
  334.3 0.1 copy.26
  334.4 17.8 %all_to_all.55 = bf16[8,512,128]{2,1,0:T(8,128)(2,1)S(1)} all-to-all(bf16[8,512,128]{2,1,0:T(8,128)(2,1)S(1)} %bitcast.44), channel_id=1, replica_groups=mesh['rep'=8,'tp'=16] {'rep'}, dimensions={0} | all-to-all | bytes 2097152 | tf_op jit(solution)/shard_map/all_to_all | solution.py:84
  352.1 0.0 all-gather.6.cloned.1.call-done
  352.1 7.3 %maximum_select_fusion = bf16[4096,1024]{1,0:T(8,128)(2,1)} fusion(bf16[4096,128]{1,0:T(8,128)(2,1)S(1)} %bitcast.42, bf16[4096,896]{1,0:T(8,128)(2,1)} %all-gather.6.cloned.1.call-done, pred[]{:T(512)S(6)} %eq.59), kind=kLoop, calls=%fused_computation.1 | loop fusion | flops 20971520 | bytes 16777216 | tf_op jit(solution)/shard_map/jit(_where)/select_n | solution.py:86
  (11 shorter events, 0.2 us)
Async XLA Ops:
  7.2 10.3 %copy-start.3 = (s32[1,384]{1,0:T(1,128)S(1)}, s32[1,384]{1,0:T(1,128)}, u32[]{:S(2)}) copy-start(s32[1,384]{1,0:T(1,128)} %param.10) | copy-start | bytes 4612
  9.3 76.3 %copy-start.5 = (bf16[384,1024]{1,0:T(8,128)(2,1)S(1)}, bf16[384,1024]{1,0:T(8,128)(2,1)}, u32[]{:S(2)}) copy-start(bf16[384,1024]{1,0:T(8,128)(2,1)} %param.14) | copy-start | bytes 2359300
  9.3 76.3 %copy-start.6 = (bf16[384,1024]{1,0:T(8,128)(2,1)S(1)}, bf16[384,1024]{1,0:T(8,128)(2,1)}, u32[]{:S(2)}) copy-start(bf16[384,1024]{1,0:T(8,128)(2,1)} %param.13) | copy-start | bytes 2359300
  9.3 23.3 %all-to-all-start = ((bf16[96,16,256]{2,0,1:T(8,128)(2,1)}), bf16[96,16,256]{2,0,1:T(8,128)(2,1)S(1)}, u32[]{:S(2)}, u32[]{:S(2)}) async-start(bf16[96,16,256]{2,0,1:T(8,128)(2,1)} %bitcast.40), calls=%async_computation | async-start | bytes 1572864 | tf_op jit(solution)/shard_map/all_to_all | solution.py:35
  17.4 68.2 %all-gather.4.cloned.1.call-start = ((), (), s32[]{:S(2)}) async-start(), calls=%async_computation.6 | async-start | bytes 3342336 | tf_op jit(solution)/shard_map/all_gather | solution.py:37
  95.3 3.9 %copy-start.2 = (s32[1,16]{1,0:T(1,128)S(1)}, s32[1,16]{1,0:T(1,128)}, u32[]{:S(2)}) copy-start(s32[1,16]{1,0:T(1,128)} %param.11) | copy-start | bytes 196
  95.3 27.5 %all-to-all-start.1 = ((bf16[16,384,128]{2,1,0:T(8,128)(2,1)}), bf16[16,384,128]{2,1,0:T(8,128)(2,1)S(1)}, u32[]{:S(2)}, u32[]{:S(2)}) async-start(bf16[16,384,128]{2,1,0:T(8,128)(2,1)} %broadcast_in_dim.53), calls=%async_computation.1 | async-start | bytes 3145728 | tf_op jit(solution)/shard_map/all_to_all | solution.py:47
  99.2 115.1 %reduce-scatter.2.cloned.1.call-start = ((), (), s32[]{:S(2)}) async-start(), calls=%async_computation.7 | async-start | bytes 8257536 | tf_op jit(solution)/shard_map/reduce_scatter | solution.py:67
  122.8 3.2 copy-start.4
  132.4 81.8 %copy-start = (f32[512,896]{1,0:T(8,128)S(1)}, f32[512,896]{1,0:T(8,128)}, u32[]{:S(2)}) copy-start(f32[512,896]{1,0:T(8,128)} %param.15) | copy-start | bytes 5505028
  132.4 81.8 %copy-start.1 = (bf16[512,896]{1,0:T(8,128)(2,1)S(1)}, bf16[512,896]{1,0:T(8,128)(2,1)}, u32[]{:S(2)}) copy-start(bf16[512,896]{1,0:T(8,128)(2,1)} %param.17) | copy-start | bytes 2752516
  132.5 219.7 %all-gather.6.cloned.1.call-start = ((), (), s32[]{:S(2)}) async-start(), calls=%async_computation.8 | async-start | bytes 8257536 | tf_op jit(solution)/shard_map/all_gather | solution.py:75
  220.0 89.6 %all-to-all-start.2 = ((bf16[16,32,896]{2,1,0:T(8,128)(2,1)}), bf16[16,32,896]{2,1,0:T(8,128)(2,1)S(1)}, u32[]{:S(2)}, u32[]{:S(2)}) async-start(bf16[16,32,896]{2,1,0:T(8,128)(2,1)} %bitcast.41), calls=%async_computation.3 | async-start | bytes 1835008 | tf_op jit(solution)/shard_map/all_to_all | solution.py:78
Sparse Core Ops, SparseCore 0:
  33.9 51.5 all-gather.3
  132.6 81.6 reduce-scatter.1
  220.1 88.2 all-gather.5
where the time goes:
time: 367 us; the launch traced here: 366 us
  waiting for transfers between devices  232 us (63%)
  blocking collectives  61.1 us (17%)
  starting transfers between devices  18.8 us (5%)
  other arithmetic  17.5 us (5%)
  matrix products  16.4 us (4%)
  between operations  14.6 us (4%)
  local copies, waits for them, and re-layouts  6.07 us (2%)
    reduce_scatter x1, waiting for transfers between devices, on_device(): lax.psum_scatter((product * scaling).astype(jnp.bfloat16), 'rep', scatter...  81.7 us
    all_to_all x1, waiting for transfers between devices, on_device(): lax.all_to_all(fresh, 'tp', split_axis=0, concat_axis=0, tiled=True)  60.8 us
    all_gather x1, waiting for transfers between devices, on_device(): inputs = lax.all_gather(chosen, 'tp', axis=1, tiled=True)  51.7 us
    all_to_all x1, blocking collectives, on_device(): lax.all_to_all(routed, 'tp', split_axis=1, concat_axis=2, tiled=True)  22.6 us
    all_to_all x1, waiting for transfers between devices, on_device(): lax.all_to_all(jnp.broadcast_to(gate_grad[:, wide_cols:], (tp_count, toke...  22.1 us
    all_gather x1, blocking collectives, on_device(): all_holders = lax.all_gather(holders, 'rep')  20.7 us
    all_to_all x1, blocking collectives, on_device(): lax.all_to_all(routed, 'rep', split_axis=0, concat_axis=0, tiled=True)  17.8 us
    all_to_all x1, waiting for transfers between devices, on_device(): lax.all_to_all(batch_rows, 'tp', split_axis=1, concat_axis=0, tiled=True)  15.1 us
  transfers between devices with their start and end apart: 6, of which 5 were waited for; matrix products, arithmetic and copies ran while one was open for 1% of the time, Pallas kernels for 0%

commit v1 on v0

--- a/solution.py
+++ b/solution.py
@@ -34,7 +34,9 @@
     scaling = 1.0 / math.sqrt(copies.shape[0])
     columns = lax.all_to_all(batch_rows, "tp", split_axis=1, concat_axis=0, tiled=True)
     chosen = picked(token_slots[0], columns)
-    inputs = lax.all_gather(chosen, "tp", axis=1, tiled=True)
+    inputs = jnp.concatenate(
+        lax.all_to_all(jnp.stack([chosen] * lax.axis_size("tp")), "tp", 0, 0), axis=1
+    )
     gate_pre = jnp.dot(inputs, copies, preferred_element_type=jnp.float32) * scaling
     logistic = jax.nn.sigmoid(gate_pre)
     gate_grad = (

time: 367 us -> 354 us (0.965)
  waiting for transfers between devices: 232 us -> 180 us
  blocking collectives: 61.1 us -> 104 us
  matrix products: 16.4 us -> 11.4 us
    all_gather x1 -> x0, waiting for transfers between devices: 51.7 us -> none  [on_device(): inputs = lax.all_gather(chosen, 'tp', axis=1, tiled=True)]
    all_to_all x0 -> x1, blocking collectives: none -> 43.5 us  [on_device(): lax.all_to_all(jnp.stack([chosen] * lax.axis_size('tp')), 'tp', 0, 0)]
    dot_general x1, matrix products: 8.27 us -> 3.95 us  [on_device(): jnp.dot(inputs, copies, preferred_element_type=jnp.float32) * scaling]
  transfers between devices with their start and end apart: 6 -> 5, of which waited for: 5 -> 4; matrix products, arithmetic and copies ran while one was open for 1% -> 1% of each run, Pallas kernels for 0% -> 0%
where the time goes in v1:
time: 354 us; the launch traced here: 353 us
  waiting for transfers between devices  180 us (51%)
  blocking collectives  104 us (29%)
  starting transfers between devices  18.6 us (5%)
  other arithmetic  17.5 us (5%)
  between operations  14.9 us (4%)
  matrix products  11.4 us (3%)
  local copies, waits for them, and re-layouts  6.64 us (2%)
    reduce_scatter x1, waiting for transfers between devices, on_device(): lax.psum_scatter((product * scaling).astype(jnp.bfloat16), 'rep', scatter...  81.4 us
    all_to_all x1, waiting for transfers between devices, on_device(): lax.all_to_all(fresh, 'tp', split_axis=0, concat_axis=0, tiled=True)  60.8 us
    all_to_all x1, blocking collectives, on_device(): lax.all_to_all(jnp.stack([chosen] * lax.axis_size('tp')), 'tp', 0, 0)  43.5 us
    all_to_all x1, blocking collectives, on_device(): lax.all_to_all(routed, 'tp', split_axis=1, concat_axis=2, tiled=True)  22.6 us
    all_to_all x1, waiting for transfers between devices, on_device(): lax.all_to_all(jnp.broadcast_to(gate_grad[:, wide_cols:], (tp_count, toke...  22.1 us
    all_gather x1, blocking collectives, on_device(): all_holders = lax.all_gather(holders, 'rep')  20.6 us
    all_to_all x1, blocking collectives, on_device(): lax.all_to_all(routed, 'rep', split_axis=0, concat_axis=0, tiled=True)  17.8 us
    all_to_all x1, waiting for transfers between devices, on_device(): lax.all_to_all(batch_rows, 'tp', split_axis=1, concat_axis=0, tiled=True)  15.1 us
  transfers between devices with their start and end apart: 5, of which 4 were waited for; matrix products, arithmetic and copies ran while one was open for 1% of the time, Pallas kernels for 0%

profile of v1, /device:TPU:0, one launch (start us, length us, event | category | flops | bytes accessed | tf_op | source)
XLA Modules:
  0.0 353.0 jit_solution(14420702355481920342)
XLA Ops:
  7.2 0.0 copy-start.5
  7.2 2.1 copy.40
  9.3 8.0 %all-to-all-start = ((bf16[96,16,256]{2,0,1:T(8,128)(2,1)}), bf16[96,16,256]{2,0,1:T(8,128)(2,1)S(1)}, u32[]{:S(2)}, u32[]{:S(2)}) async-start(bf16[96,16,256]{2,0,1:T(8,128)(2,1)} %bitcast.43), calls=%async_computation | async-start | bytes 1572864 | tf_op jit(solution)/shard_map/all_to_all | solution.py:35
  17.3 0.0 copy-done.5
  17.3 15.1 %all-to-all-done = bf16[96,16,256]{2,0,1:T(8,128)(2,1)S(1)} async-done(((bf16[96,16,256]{2,0,1:T(8,128)(2,1)}), bf16[96,16,256]{2,0,1:T(8,128)(2,1)S(1)}, u32[]{:S(2)}, u32[]{:S(2)}) %all-to-all-start) | async-done | bytes 786464 | tf_op jit(solution)/shard_map/all_to_all | solution.py:35
  32.4 0.6 fusion.7
  33.0 0.0 copy-start.8
  33.0 0.2 copy.28
  33.2 0.0 copy-start.6
  33.2 0.4 stack.2
  33.6 0.0 copy-start.7
  33.6 43.5 %all_to_all.59 = bf16[16,384,256]{1,2,0:T(8,128)(2,1)S(1)} all-to-all(bf16[16,384,256]{1,2,0:T(8,128)(2,1)S(1)} %stack.2), channel_id=1, replica_groups=mesh['rep'=8,'tp'=16] {'tp'}, dimensions={0} | all-to-all | bytes 6291456 | tf_op jit(solution)/shard_map/all_to_all | solution.py:38
  77.1 0.0 copy-start
  77.1 0.0 copy-done.8
  77.1 0.0 copy-done.6
  77.1 0.0 copy-done.7
  77.1 4.0 %multiply_convert_fusion.1 = bf16[384,1024]{1,0:T(8,128)(2,1)S(1)} fusion(bf16[384,1024]{1,0:T(8,128)(2,1)S(1)} %copy-done.7, bf16[384,1024]{1,0:T(8,128)(2,1)S(1)} %copy-done.8, bf16[384,4096]{0,1:T(8,128)(2,1)S(1)} %bitcast.50, bf16[4096,1024]{1,0:T(8,128)(2,1)S(1)} %copy-done.6), kind=kOutput, calls=%fused_computation.17 | convolution fusion | flops 3226337280 | bytes 13893632 | tf_op jit(solution)/shard_map/dot_general | solution.py:40
  81.1 0.0 copy-done
  81.1 1.4 broadcast_in_dim.53
  82.6 0.0 copy-start.4
  82.6 3.8 %all-to-all-start.2 = ((bf16[16,384,128]{2,1,0:T(8,128)(2,1)}), bf16[16,384,128]{2,1,0:T(8,128)(2,1)S(1)}, u32[]{:S(2)}, u32[]{:S(2)}) async-start(bf16[16,384,128]{2,1,0:T(8,128)(2,1)} %broadcast_in_dim.53), calls=%async_computation.2 | async-start | bytes 3145728 | tf_op jit(solution)/shard_map/all_to_all | solution.py:49
  86.4 0.0 reduce-scatter.2.cloned.1.call-start
  86.5 0.0 copy-done.4
  86.5 0.6 fusion.12
  87.8 0.1 compare_convert_fusion
  87.9 22.1 %all-to-all-done.2 = bf16[16,384,128]{2,1,0:T(8,128)(2,1)S(1)} async-done(((bf16[16,384,128]{2,1,0:T(8,128)(2,1)}), bf16[16,384,128]{2,1,0:T(8,128)(2,1)S(1)}, u32[]{:S(2)}, u32[]{:S(2)}) %all-to-all-start.2) | async-done | bytes 1572896 | tf_op jit(solution)/shard_map/all_to_all | solution.py:49
  110.0 0.0 copy-start.1
  110.0 3.0 select_reduce_fusion
  113.2 0.0 copy-done.1
  113.2 6.4 %multiply_convert_fusion = bf16[4096,896]{1,0:T(8,128)(2,1)} fusion(bf16[384,4096]{0,1:T(8,128)(2,1)S(1)} %bitcast.51, bf16[384,896]{1,0:T(8,128)(2,1)S(1)} %constant_dynamic-update-slice_fusion, bf16[384,1024]{1,0:T(8,128)(2,1)S(1)} %multiply_convert_fusion.1, pred[]{:T(512)S(6)} %eq.59), kind=kOutput, calls=%fused_computation | convolution fusion | flops 2826256384 | bytes 11862017 | tf_op jit(solution)/shard_map/dot_general | solution.py:66
  119.6 0.0 copy-start.2
  119.6 0.0 copy-start.3
  119.6 0.0 reduce-scatter.2.cloned.1.call-update
  119.6 0.0 all-gather.3.cloned.1.call-start
  119.7 81.4 %reduce-scatter.2.cloned.1.call-done = bf16[512,896]{1,0:T(8,128)(2,1)} async-done(((bf16[4096,896]{1,0:T(8,128)(2,1)}), bf16[512,896]{1,0:T(8,128)(2,1)}) %reduce-scatter.2.cloned.1.call-update) | async-done | bytes 917520 | tf_op jit(solution)/shard_map/reduce_scatter | solution.py:69
  201.0 0.0 copy-done.2
  201.0 0.0 copy-done.3
  201.0 5.7 %fusion.13 = (bf16[512,896]{1,0:T(8,128)(2,1)}, f32[512,896]{1,0:T(8,128)}, bf16[512,896]{1,0:T(8,128)(2,1)}, bf16[512,896]{1,0:T(8,128)(2,1)}) fusion(f32[512,896]{1,0:T(8,128)S(1)} %copy-done.2, bf16[512,896]{1,0:T(8,128)(2,1)S(1)} %copy-done.3, bf16[512,896]{1,0:T(8,128)(2,1)} %reduce-scatter.2.cloned.1.call-done, bf16[512,896]{1,0:T(8,128)(2,1)} %param.16), kind=kLoop, calls=%fused_computation.48 | loop fusion | flops 9633792 | bytes 9175040 | tf_op jit(solution)/shard_map/convert_element_type | solution.py:76
  206.8 0.0 all-gather.3.cloned.1.call-update
  206.8 6.7 %all-to-all-start.3 = ((bf16[16,32,896]{2,1,0:T(8,128)(2,1)}), bf16[16,32,896]{2,1,0:T(8,128)(2,1)S(1)}, u32[]{:S(2)}, u32[]{:S(2)}) async-start(bf16[16,32,896]{2,1,0:T(8,128)(2,1)} %bitcast.44), calls=%async_computation.4 | async-start | bytes 1835008 | tf_op jit(solution)/shard_map/all_to_all | solution.py:80
  213.5 20.6 %all-gather = s32[8,1,16]{2,1,0:T(1,128)S(1)} all-gather(s32[1,1,16]{2,1,0:T(1,128)S(1)} %bitcast.55), channel_id=1, replica_groups=mesh['rep'=8,'tp'=16] {'rep'}, dimensions={0}, use_global_device_ids=true | all-gather | bytes 576 | tf_op jit(solution)/shard_map/all_gather | solution.py:31
  234.1 0.6 broadcast.94
  234.7 0.7 reduce.11
  235.4 0.1 eq.63
  235.5 60.8 %all-to-all-done.3 = bf16[16,32,896]{2,1,0:T(8,128)(2,1)S(1)} async-done(((bf16[16,32,896]{2,1,0:T(8,128)(2,1)}), bf16[16,32,896]{2,1,0:T(8,128)(2,1)S(1)}, u32[]{:S(2)}, u32[]{:S(2)}) %all-to-all-start.3) | async-done | bytes 917536 | tf_op jit(solution)/shard_map/all_to_all | solution.py:80
  296.3 1.0 reshape.110
  297.4 0.2 copy.29
  297.5 0.5 fusion.5
  298.0 0.2 copy.34
  298.3 0.1 copy.30
  298.4 22.6 %all_to_all.60 = bf16[8,16,32,128]{3,2,0,1:T(8,128)(2,1)S(1)} all-to-all(bf16[8,16,32,128]{3,2,0,1:T(8,128)(2,1)S(1)} %copy.30), channel_id=1, replica_groups=mesh['rep'=8,'tp'=16] {'tp'}, dimensions={1} | all-to-all | bytes 2097152 | tf_op jit(solution)/shard_map/all_to_all | solution.py:84
  321.0 0.1 copy.31
  321.1 17.8 %all_to_all.61 = bf16[8,512,128]{2,1,0:T(8,128)(2,1)S(1)} all-to-all(bf16[8,512,128]{2,1,0:T(8,128)(2,1)S(1)} %bitcast.47), channel_id=1, replica_groups=mesh['rep'=8,'tp'=16] {'rep'}, dimensions={0} | all-to-all | bytes 2097152 | tf_op jit(solution)/shard_map/all_to_all | solution.py:86
  338.9 0.0 all-gather.3.cloned.1.call-done
  338.9 7.3 %maximum_select_fusion = bf16[4096,1024]{1,0:T(8,128)(2,1)} fusion(bf16[4096,128]{1,0:T(8,128)(2,1)S(1)} %bitcast.45, bf16[4096,896]{1,0:T(8,128)(2,1)} %all-gather.3.cloned.1.call-done, pred[]{:T(512)S(6)} %eq.59), kind=kLoop, calls=%fused_computation.1 | loop fusion | flops 20971520 | bytes 16777216 | tf_op jit(solution)/shard_map/jit(_where)/select_n | solution.py:88
  (11 shorter events, 0.2 us)
Async XLA Ops:
  7.2 10.1 %copy-start.5 = (s32[1,384]{1,0:T(1,128)S(1)}, s32[1,384]{1,0:T(1,128)}, u32[]{:S(2)}) copy-start(s32[1,384]{1,0:T(1,128)} %param.10) | copy-start | bytes 4612
  9.3 23.2 %all-to-all-start = ((bf16[96,16,256]{2,0,1:T(8,128)(2,1)}), bf16[96,16,256]{2,0,1:T(8,128)(2,1)S(1)}, u32[]{:S(2)}, u32[]{:S(2)}) async-start(bf16[96,16,256]{2,0,1:T(8,128)(2,1)} %bitcast.43), calls=%async_computation | async-start | bytes 1572864 | tf_op jit(solution)/shard_map/all_to_all | solution.py:35
  33.0 44.1 %copy-start.8 = (bf16[384,1024]{1,0:T(8,128)(2,1)S(1)}, bf16[384,1024]{1,0:T(8,128)(2,1)}, u32[]{:S(2)}) copy-start(bf16[384,1024]{1,0:T(8,128)(2,1)} %param.13) | copy-start | bytes 2359300
  33.2 43.9 %copy-start.6 = (bf16[4096,1024]{1,0:T(8,128)(2,1)S(1)}, bf16[4096,1024]{1,0:T(8,128)(2,1)}, u32[]{:S(2)}) copy-start(bf16[4096,1024]{1,0:T(8,128)(2,1)} %param.12) | copy-start | bytes 25165828
  33.6 43.5 %copy-start.7 = (bf16[384,1024]{1,0:T(8,128)(2,1)S(1)}, bf16[384,1024]{1,0:T(8,128)(2,1)}, u32[]{:S(2)}) copy-start(bf16[384,1024]{1,0:T(8,128)(2,1)} %param.14) | copy-start | bytes 2359300
  77.1 4.0 %copy-start = (bf16[16,384,256]{1,2,0:T(8,128)(2,1)}, bf16[16,384,256]{1,2,0:T(8,128)(2,1)S(1)}, u32[]{:S(2)}) copy-start(bf16[16,384,256]{1,2,0:T(8,128)(2,1)S(1)} %all_to_all.59) | copy-start | bytes 9437188
  82.6 3.9 %copy-start.4 = (s32[1,16]{1,0:T(1,128)S(1)}, s32[1,16]{1,0:T(1,128)}, u32[]{:S(2)}) copy-start(s32[1,16]{1,0:T(1,128)} %param.11) | copy-start | bytes 196
  82.6 27.4 %all-to-all-start.2 = ((bf16[16,384,128]{2,1,0:T(8,128)(2,1)}), bf16[16,384,128]{2,1,0:T(8,128)(2,1)S(1)}, u32[]{:S(2)}, u32[]{:S(2)}) async-start(bf16[16,384,128]{2,1,0:T(8,128)(2,1)} %broadcast_in_dim.53), calls=%async_computation.2 | async-start | bytes 3145728 | tf_op jit(solution)/shard_map/all_to_all | solution.py:49
  86.4 114.6 %reduce-scatter.2.cloned.1.call-start = ((), (), s32[]{:S(2)}) async-start(), calls=%async_computation.7 | async-start | bytes 8257536 | tf_op jit(solution)/shard_map/reduce_scatter | solution.py:69
  110.0 3.2 copy-start.1
  119.6 81.5 %copy-start.2 = (f32[512,896]{1,0:T(8,128)S(1)}, f32[512,896]{1,0:T(8,128)}, u32[]{:S(2)}) copy-start(f32[512,896]{1,0:T(8,128)} %param.15) | copy-start | bytes 5505028
  119.6 81.5 %copy-start.3 = (bf16[512,896]{1,0:T(8,128)(2,1)S(1)}, bf16[512,896]{1,0:T(8,128)(2,1)}, u32[]{:S(2)}) copy-start(bf16[512,896]{1,0:T(8,128)(2,1)} %param.17) | copy-start | bytes 2752516
  119.6 219.3 %all-gather.3.cloned.1.call-start = ((), (), s32[]{:S(2)}) async-start(), calls=%async_computation.8 | async-start | bytes 8257536 | tf_op jit(solution)/shard_map/all_gather | solution.py:77
  206.8 89.5 %all-to-all-start.3 = ((bf16[16,32,896]{2,1,0:T(8,128)(2,1)}), bf16[16,32,896]{2,1,0:T(8,128)(2,1)S(1)}, u32[]{:S(2)}, u32[]{:S(2)}) async-start(bf16[16,32,896]{2,1,0:T(8,128)(2,1)} %bitcast.44), calls=%async_computation.4 | async-start | bytes 1835008 | tf_op jit(solution)/shard_map/all_to_all | solution.py:80
Sparse Core Ops, SparseCore 0:
  119.7 81.2 reduce-scatter.1
  206.9 88.1 all-gather.2
